TPU v7x, 32 devices: a whole 2x2x4 slice. The times are simulated.
32 devices in a mesh: ctx: 16 (over z, x, core), head: 2 (over y).
Axes of the slice: x: 2, y: 2, z: 4, core: 2. Of those that a mesh axis runs over, the one named last changes fastest.
Arguments:
- query_rows: bfloat16 [8192, 2048], P('ctx', 'head'), may hold values from -60 to 60
- key_rows: bfloat16 [8192, 2048], P('ctx', 'head'), may hold values from -6 to 6
- value_rows: bfloat16 [8192, 2048], P('ctx', 'head'), may hold values from -60 to 60
- log_gate: float32 [16, 8192], P('head', 'ctx'), may hold values from -0.5 to 0
- conv_weight: float32 [3, 4, 2048], P(None, None, 'head'), may hold values from -3 to 3
- norm_gain: float32 [2048], P('head'), may hold values from 0.5 to 1.5
- mixed_grad: bfloat16 [8192, 2048], P('ctx', 'head'), may hold values from -24 to 24
Outputs:
- mixer_out: bfloat16 [8192, 2048], P('ctx', 'head')
- query_grad: bfloat16 [8192, 2048], P('ctx', 'head')
- key_grad: bfloat16 [8192, 2048], P('ctx', 'head')
- value_grad: bfloat16 [8192, 2048], P('ctx', 'head')
- conv_grad: float32 [3, 4, 2048], P(None, None, 'head')
- gain_grad: float32 [2048], P('head')
All inputs are finite; a program needn't handle non-finite values.
Results may differ from a plain program's by a relative error of at most 0.015.
Values may be sent and summed in bfloat16 or wider, within the bound.
A program may use at most 128 MiB of HBM per device.

v0:
```python
import jax
import jax.numpy as jnp
from jax import lax
from jax.sharding import PartitionSpec as P

HD = 128
TAPS = 4
GROUP = 512
D = 2048
norm_epsilon = 1e-05


def shifted(block, axis, distance):
    devices = range(lax.axis_size(axis))
    route = [(i - distance, i) for i in devices if i - distance in devices]
    return lax.ppermute(block, axis, route)


def prefix(value, axis, join, neutral):
    count = lax.axis_size(axis)
    place = lax.axis_index(axis)
    ahead = count - 1 - place
    gathered = jax.tree.map(
        lambda a, kind: lax.all_gather(a.astype(kind), axis), value, (jnp.bfloat16, jnp.bfloat16)
    )
    state = jax.tree.map(lambda a, e: jnp.zeros_like(a) + jnp.asarray(e, a.dtype), value, neutral)

    def one(turn, state):
        source = count - 1 - turn
        return join(
            state,
            jax.tree.map(
                lambda a, own: lax.dynamic_index_in_dim(a, source, 0, False).astype(own.dtype),
                gathered,
                value,
            ),
        )

    return lax.fori_loop(0, ahead, one, state)


def rounded(values):
    return values.astype(jnp.bfloat16)


def decay_tables(gate_blocks):
    running = jnp.cumsum(gate_blocks, axis=-1)
    closing = running[..., -1]
    gap_matrix = running[..., :, None] - running[..., None, :]
    block_size = gate_blocks.shape[-1]
    lower_mask = jnp.arange(block_size)[:, None] >= jnp.arange(block_size)[None, :]
    weights = jnp.where(lower_mask, jnp.exp(jnp.minimum(gap_matrix, 0.0)), 0.0)
    return (running, closing, weights)


def chain_step(earlier, later_part):
    return (
        earlier[0] + later_part[0],
        jnp.exp(later_part[0])[..., None, None] * earlier[1] + later_part[1],
    )


def local_chain(closing, blocks, backwards):

    def advance(partial_sum, block_item):
        return (chain_step(partial_sum, block_item), partial_sum)

    initial = (jnp.zeros(closing.shape[1:], jnp.float32), jnp.zeros(blocks.shape[1:], jnp.float32))
    return lax.scan(advance, initial, (closing, blocks), reverse=backwards)


def conv_forward(rim_rows, rows, weight, tok_here):
    extended = jnp.concatenate([rim_rows, rows], axis=0).astype(jnp.float32)
    result = weight[0][None, :] * extended[TAPS - 1 : TAPS - 1 + tok_here]
    for offset in range(1, TAPS):
        result = (
            result
            + weight[offset][None, :] * extended[TAPS - 1 - offset : TAPS - 1 - offset + tok_here]
        )
    return (rounded(result), extended)


def conv_backward(grad_rows, edge_rows, extended, weight, tok_here):
    ahead_all = jnp.concatenate([grad_rows, edge_rows], axis=0)
    input_grad = weight[0][None, :] * grad_rows
    weight_grad = [jnp.sum(grad_rows * extended[TAPS - 1 : TAPS - 1 + tok_here], axis=0)]
    for offset in range(1, TAPS):
        input_grad = input_grad + weight[offset][None, :] * ahead_all[offset : offset + tok_here]
        weight_grad.append(
            jnp.sum(grad_rows * extended[TAPS - 1 - offset : TAPS - 1 - offset + tok_here], axis=0)
        )
    return (rounded(input_grad), jnp.stack(weight_grad))


def body(query_rows, key_rows, value_rows, log_gate, conv_weight, norm_gain, mixed_grad):
    tok_here = query_rows.shape[0]
    width_here = query_rows.shape[1]
    heads_here = width_here // HD
    block_count = tok_here // GROUP
    rim_rows = shifted(
        jnp.stack(
            [
                query_rows[tok_here - (TAPS - 1) :],
                key_rows[tok_here - (TAPS - 1) :],
                value_rows[tok_here - (TAPS - 1) :],
            ]
        ),
        "ctx",
        1,
    )
    query_conv, query_ext = conv_forward(rim_rows[0], query_rows, conv_weight[0], tok_here)
    key_conv, key_ext = conv_forward(rim_rows[1], key_rows, conv_weight[1], tok_here)
    value_conv, value_ext = conv_forward(rim_rows[2], value_rows, conv_weight[2], tok_here)
    query_blocks = query_conv.reshape(block_count, GROUP, heads_here, HD)
    key_blocks = key_conv.reshape(block_count, GROUP, heads_here, HD)
    value_blocks = value_conv.reshape(block_count, GROUP, heads_here, HD)
    gate_blocks = log_gate.reshape(heads_here, block_count, GROUP).transpose(1, 0, 2)
    running, closing, weights = decay_tables(gate_blocks)
    grow_factor = jnp.exp(running).transpose(0, 2, 1)[..., None]
    shrink = jnp.exp(closing[..., None] - running).transpose(0, 2, 1)[..., None]
    scores = jnp.einsum(
        "nthd,nshd->nhts", query_blocks, key_blocks, preferred_element_type=jnp.float32
    )
    weights_low = rounded(scores * weights)
    key_scaled = rounded(key_blocks * shrink)
    blocks = jnp.einsum(
        "nshd,nshe->nhde", key_scaled, value_blocks, preferred_element_type=jnp.float32
    )
    device_sum, before = local_chain(closing, blocks, False)
    zero_state = jnp.zeros((heads_here, HD, HD), jnp.float32)
    all_totals = lax.all_gather(device_sum[0][None], "ctx", axis=0, tiled=True)
    device_index = lax.axis_index("ctx")
    cumulative = jnp.cumsum(all_totals, axis=0)
    before_me = cumulative[device_index] - all_totals[device_index]
    sources = jnp.arange(all_totals.shape[0])
    factor_table = jnp.where(
        (sources < device_index)[:, None],
        jnp.exp(jnp.minimum(before_me[None, :] - cumulative, 0.0)),
        0.0,
    )
    incoming = jnp.einsum(
        "nh,nhde->hde",
        factor_table,
        lax.all_gather(device_sum[1][None], "ctx", axis=0, tiled=True),
        precision=lax.Precision.HIGHEST,
    )
    group_in = jnp.exp(before[0])[..., None, None] * incoming[None] + before[1]
    state_low = rounded(group_in)
    attended = jnp.einsum(
        "nhts,nshe->nthe", weights_low, value_blocks, preferred_element_type=jnp.float32
    )
    attended = (
        attended
        + jnp.einsum("nthd,nhde->nthe", query_blocks, state_low, preferred_element_type=jnp.float32)
        * grow_factor
    )
    attended = attended.reshape(tok_here, width_here)
    grad_wide = mixed_grad.astype(jnp.float32)
    scaled = grad_wide * norm_gain[None, :]
    squares = lax.psum(jnp.sum(attended * attended, axis=1), "head")
    inverse = lax.rsqrt(squares / D + norm_epsilon)
    inner_sum = lax.psum(jnp.sum(scaled * attended, axis=1), "head") / D
    normed = attended * inverse[:, None]
    mixer_out = rounded(normed * norm_gain[None, :])
    gain_part = jnp.sum(grad_wide * normed, axis=0)
    out_grad = rounded(
        inverse[:, None] * (scaled - attended * (inverse * inverse * inner_sum)[:, None])
    )
    grad_blocks = out_grad.reshape(block_count, GROUP, heads_here, HD)
    grad_scores = rounded(
        jnp.einsum("nthe,nshe->nhts", grad_blocks, value_blocks, preferred_element_type=jnp.float32)
        * weights
    )
    query_scaled = rounded(query_blocks * grow_factor)
    back_blocks = jnp.einsum(
        "nthd,nthe->nhde", query_scaled, grad_blocks, preferred_element_type=jnp.float32
    )
    back_sum, back_before = local_chain(closing, back_blocks, True)
    later_state = prefix(
        (back_sum[0], back_sum[1]),
        "ctx",
        chain_step,
        (jnp.zeros((heads_here,), jnp.float32), zero_state),
    )[1]
    later_low = rounded(
        jnp.exp(back_before[0])[..., None, None] * later_state[None] + back_before[1]
    )
    query_cg = jnp.einsum(
        "nhts,nshd->nthd", grad_scores, key_blocks, preferred_element_type=jnp.float32
    )
    query_cg = (
        query_cg
        + jnp.einsum("nthe,nhde->nthd", grad_blocks, state_low, preferred_element_type=jnp.float32)
        * grow_factor
    )
    key_cg = jnp.einsum(
        "nhts,nthd->nshd", grad_scores, query_blocks, preferred_element_type=jnp.float32
    )
    key_cg = (
        key_cg
        + jnp.einsum("nshe,nhde->nshd", value_blocks, later_low, preferred_element_type=jnp.float32)
        * shrink
    )
    value_cg = jnp.einsum(
        "nhts,nthe->nshe", weights_low, grad_blocks, preferred_element_type=jnp.float32
    )
    value_cg = (
        value_cg
        + jnp.einsum("nshd,nhde->nshe", key_blocks, later_low, preferred_element_type=jnp.float32)
        * shrink
    )
    query_cg = query_cg.reshape(tok_here, width_here)
    key_cg = key_cg.reshape(tok_here, width_here)
    value_cg = value_cg.reshape(tok_here, width_here)
    edge_rows = shifted(
        jnp.stack([query_cg[: TAPS - 1], key_cg[: TAPS - 1], value_cg[: TAPS - 1]]), "ctx", -1
    )
    query_grad, query_taps = conv_backward(
        query_cg, edge_rows[0], query_ext, conv_weight[0], tok_here
    )
    key_grad, key_taps = conv_backward(key_cg, edge_rows[1], key_ext, conv_weight[1], tok_here)
    value_grad, value_taps = conv_backward(
        value_cg, edge_rows[2], value_ext, conv_weight[2], tok_here
    )
    conv_part = jnp.stack([query_taps, key_taps, value_taps])
    conv_grad, gain_grad = lax.psum((conv_part, gain_part), "ctx")
    return (mixer_out, query_grad, key_grad, value_grad, conv_grad, gain_grad)


def solution(mesh):
    placed = (
        P("ctx", "head"),
        P("ctx", "head"),
        P("ctx", "head"),
        P("head", "ctx"),
        P(None, None, "head"),
        P("head"),
        P("ctx", "head"),
    )
    return jax.shard_map(
        body,
        mesh=mesh,
        in_specs=placed,
        out_specs=(
            P("ctx", "head"),
            P("ctx", "head"),
            P("ctx", "head"),
            P("ctx", "head"),
            P(None, None, "head"),
            P("head"),
        ),
        check_vma=False,
    )
```

profile of v0, /device:TPU:0, one launch (start us, length us, event | category | flops | bytes accessed | tf_op | source)
XLA Modules:
  0.0 309.8 jit_solution(4000271757423066720)
XLA Ops:
  8.8 2.4 collective-permute-start
  11.2 2.2 reduce-window.6
  16.5 1.7 maximum_convert_fusion
  19.7 1.5 copy.163
  21.2 4.9 %fusion.49 = bf16[64,8,8,128]{3,2,1,0:T(8,128)(2,1)S(1)} fusion(f32[515,1024]{1,0:T(8,128)} %maximum_convert_fusion, f32[1024]{0:T(1024)S(1)} %bitcast.226, f32[1024]{0:T(1024)S(1)} %bitcast.228, f32[1024]{0:T(1024)S(1)} %bitcast.230, f32[1024]{0:T(1024)S(1)} %bitcast.224), kind=kLoop, calls=%fused_computation.94 | loop fusion | flops 4194304 | bytes 9453568
  26.1 1.3 convolution_add_fusion.1
  28.5 22.8 %all-gather = f32[16,8,1]{1,2,0:T(1,128)S(1)} all-gather(f32[1,8,1]{1,2,0:T(1,128)S(1)} %get-tuple-element.187), channel_id=2, replica_groups=mesh['ctx'=16,'head'=2] {'ctx'}, dimensions={0}, use_global_device_ids=true | all-gather | bytes 544 | tf_op jit(solution)/shard_map/all_gather | solution.py:131
  52.4 1.4 bitcast_add_fusion
  53.7 1.5 maximum_convert_fusion.1
  55.3 1.3 copy-done
  56.6 1.9 add_convert_fusion.1
  58.5 2.3 copy.213
  62.0 2.9 multiply_convert_fusion.1
  65.0 2.0 copy-done.2
  66.9 2.8 fusion.42
  69.8 35.3 %all-gather.7.cloned.1.call-done = f32[128,128,128]{2,1,0:T(8,128)} async-done(((f32[8,128,128]{2,1,0:T(8,128)}), f32[128,128,128]{2,1,0:T(8,128)}) %all-gather.7.cloned.1.call-update) | async-done | bytes 8388624 | tf_op jit(solution)/shard_map/all_gather | solution.py:144
  105.1 12.5 %fusion = f32[8,1,128,128]{3,1,2,0:T(1,128)S(1)} fusion(f32[16,8,1,1]{0,2,3,1:T(1,128)S(1)} %copy.206, f32[16,8,128,128]{3,2,1,0:T(8,128)} %bitcast.188), kind=kOutput, calls=%fused_computation.2 | convolution fusion | flops 25165824 | bytes 8913408 | tf_op jit(solution)/shard_map/nh,nhde->hde/dot_general | solution.py:141
  117.6 1.9 multiply_reduce_fusion.12
  119.5 5.1 %psum.28 = f32[512]{0:T(512)S(1)} all-reduce(f32[512]{0:T(512)S(1)} %get-tuple-element.206), channel_id=1, replica_groups=mesh['ctx'=16,'head'=2] {'head'}, use_global_device_ids=true, to_apply=%region_4.5 | all-reduce | flops 512 | bytes 4096 | tf_op jit(solution)/shard_map/psum | solution.py:160
  124.7 2.9 copy.169
  127.6 2.6 fusion.7
  130.2 4.9 %psum.29 = f32[512]{0:T(512)S(1)} all-reduce(f32[512]{0:T(512)S(1)} %get-tuple-element.166), channel_id=1, replica_groups=mesh['ctx'=16,'head'=2] {'head'}, use_global_device_ids=true, to_apply=%region_6.7 | all-reduce | flops 512 | bytes 4096 | tf_op jit(solution)/shard_map/psum | solution.py:162
  135.2 3.9 %fusion.6 = (bf16[512,1024]{1,0:T(8,128)(2,1)}, bf16[512,1024]{1,0:T(8,128)(2,1)}) fusion(bf16[512,1024]{1,0:T(8,128)(2,1)} %param.15, f32[512,1024]{1,0:T(8,128)} %copy.169, f32[512]{0:T(512)S(1)} %multiply_multiply_fusion, f32[1024]{0:T(1024)S(1)} %copy-done.25, f32[512]{0:T(512)S(1)} %add_rsqrt_fusion), kind=kLoop, calls=%fused_computation.19 | loop fusion | flops 4718592 | bytes 5251072 | tf_op jit(solution)/shard_map/convert_element_type | solution.py:43
  139.0 2.3 copy.214
  141.3 2.7 fusion.39
  144.0 18.6 %all-gather.3 = bf16[16,8,1]{1,2,0:T(2,128)(2,1)S(1)} all-gather(bf16[1,8,1]{1,2,0:T(2,128)(2,1)S(1)} %slice.396), channel_id=5, replica_groups=mesh['ctx'=16,'head'=2] {'ctx'}, dimensions={0}, use_global_device_ids=true | all-gather | bytes 272 | tf_op jit(solution)/shard_map/all_gather | solution.py:24
  162.7 4.0 %multiply_convert_fusion = bf16[8,512,512]{2,1,0:T(8,128)(2,1)S(1)} fusion(f32[8,512]{1,0:T(8,128)S(1)} %copy-done.27, pred[512,512]{1,0:T(8,128)(4,1)} %iota_compare_fusion, bf16[512,8,128]{0,2,1:T(8,128)(2,1)} %bitcast.185, bf16[64,8,8,128]{3,2,1,0:T(8,128)(2,1)S(1)} %fusion.49), kind=kOutput, calls=%fused_computation.4 | convolution fusion | flops 547356672 | bytes 6569984 | tf_op jit(solution)/shard_map/nthe,nshe->nhts/dot_general | solution.py:171
  166.7 1.5 fusion.62
  169.7 1.3 copy-done.5
  171.9 1.2 copy.186
  173.1 4.4 %fusion.64 = f32[8,128,512]{2,1,0:T(8,128)} fusion(bf16[512,8,128]{0,2,1:T(8,128)(2,1)S(1)} %bitcast.187, bf16[8,512,512]{2,1,0:T(8,128)(2,1)} %copy-done.2), kind=kOutput, calls=%fused_computation.139 | convolution fusion | flops 536870912 | bytes 7340032 | tf_op jit(solution)/shard_map/nhts,nthe->nshe/dot_general | solution.py:204
  177.5 2.0 fusion.63
  179.6 13.5 %all-gather.9.cloned.1.call-done = bf16[128,128,128]{2,1,0:T(8,128)(2,1)} async-done(((bf16[8,128,128]{2,1,0:T(8,128)(2,1)}), bf16[128,128,128]{2,1,0:T(8,128)(2,1)}) %all-gather.9.cloned.1.call-update) | async-done | bytes 4194320 | tf_op jit(solution)/shard_map/all_gather | solution.py:24
  193.1 17.3 %while.9 = (s32[]{:T(128)}, f32[8,128,128]{2,1,0:T(8,128)S(1)}, s32[]{:T(128)}, bf16[16,8]{1,0:T(8,128)(2,1)S(1)}, bf16[16,8,128,128]{3,2,1,0:T(8,128)(2,1)}, /*index=5*/s32[]{:T(128)}, s32[]{:T(128)}, s32[]{:T(128)}, s32[]{:T(128)}) while((s32[]{:T(128)}, f32[8,128,128]{2,1,0:T(8,128)S(1)}, s32[]{:T(128)}, bf16[16,8]{1,0:T(8,128)(2,1)S(1)}, ...), condition=%wide.region_8.9_spmd, body=%wide.region_7.8_spmd.sunk | while | flops 393230 | bytes 1310955 | solution.py:39
  193.2 1.1 convert_add_fusion.2
  196.6 1.1 convert_add_fusion.2
  210.4 2.4 fusion.35
  212.9 1.3 copy-done.6
  214.4 2.4 fusion.36
  216.8 1.3 copy-done.7
  218.4 1.6 collective-permute-start.1
  220.0 3.0 copy.176
  222.9 2.9 copy.192
  225.9 2.9 copy.190
  228.8 8.9 %multiply_reduce_fusion.3 = (f32[1024]{0:T(1024)S(1)}, f32[1024]{0:T(1024)S(1)}, f32[1024]{0:T(1024)S(1)}, f32[1024]{0:T(1024)S(1)}, bf16[512,1024]{1,0:T(8,128)(2,1)}) fusion(f32[512,1024]{1,0:T(8,128)} %copy.192, f32[515,1024]{1,0:T(8,128)} %maximum_convert_fusion, f32[3,1024]{1,0:T(4,128)S(1)} %get-tuple-element.188, f32[1024]{0:T(1024)S(1)} %bitcast.227, ...), kind=kLoop, calls=%fused_computation.62 | loop fusion | flops 9957376 | bytes 11579392 | tf_op jit(solution)/shard_map/reduce_sum | solution.py:86
  237.7 2.9 multiply_reduce_fusion.11
  240.6 2.9 multiply_reduce_fusion.7
  243.7 59.3 %all-reduce = (f32[3,4,1024]{2,1,0:T(4,128)}, f32[1024]{0:T(1024)}) all-reduce(f32[3,4,1024]{2,1,0:T(4,128)S(1)} %pad_maximum_fusion.4, f32[1024]{0:T(1024)S(1)} %get-tuple-element.165), channel_id=1, replica_groups=mesh['ctx'=16,'head'=2] {'ctx'}, use_global_device_ids=true, to_apply=%region_21.22 | all-reduce | flops 13312 | bytes 106496 | tf_op jit(solution)/shard_map/psum | solution.py:226
  (133 shorter events, 27.2 us)
Async XLA Ops:
  7.2 9.3 %copy-start.21 = (bf16[512,1024]{1,0:T(8,128)(2,1)S(1)}, bf16[512,1024]{1,0:T(8,128)(2,1)}, u32[]{:S(2)}) copy-start(bf16[512,1024]{1,0:T(8,128)(2,1)} %param.11) | copy-start | bytes 3145732
  7.2 97.9 %all-gather.7.cloned.1.call-start = ((), (), s32[]{:S(2)}) async-start(), calls=%async_computation | async-start | bytes 8912896 | tf_op jit(solution)/shard_map/all_gather | solution.py:144
  8.8 7.1 %collective-permute-start = (bf16[3,3,1024]{2,1,0:T(4,128)(2,1)S(1)}, bf16[3,3,1024]{2,1,0:T(4,128)(2,1)S(1)}, u32[]{:S(2)}, u32[]{:S(2)}) collective-permute-start(bf16[3,3,1024]{2,1,0:T(4,128)(2,1)S(1)} %pad_maximum_fusion.5), channel_id=1, source_target_pairs={{0,2},{2,4},{4,6},{6,8},{8,10},{10,12},{12,14},{14,16},{16,18},{18... | collective-permute-start | bytes 55304 | tf_op jit(solution)/shard_map/ppermute | solution.py:16
  13.6 2.1 copy-start.24
  15.7 2.5 copy-start.22
  15.8 10.3 %copy-start.28 = (f32[8]{0:T(128)}, f32[8]{0:T(128)S(1)}, u32[]{:S(2)}) copy-start(f32[8]{0:T(128)S(1)} %exponential_multiply_fusion) | copy-start | bytes 100
  21.2 4.9 %copy-start.18 = (bf16[512,8,128]{0,2,1:T(8,128)(2,1)S(1)}, bf16[512,8,128]{0,2,1:T(8,128)(2,1)}, u32[]{:S(2)}) copy-start(bf16[512,8,128]{0,2,1:T(8,128)(2,1)} %copy.163) | copy-start | bytes 3145732
  26.1 136.6 %copy-start.8 = (bf16[64,8,8,128]{3,2,1,0:T(8,128)(2,1)}, bf16[64,8,8,128]{3,2,1,0:T(8,128)(2,1)S(1)}, u32[]{:S(2)}) copy-start(bf16[64,8,8,128]{3,2,1,0:T(8,128)(2,1)S(1)} %fusion.49) | copy-start | bytes 3145732
  27.4 165.6 %all-gather.9.cloned.1.call-start = ((), (), s32[]{:S(2)}) async-start(), calls=%async_computation.1 | async-start | bytes 4456448 | tf_op jit(solution)/shard_map/all_gather | solution.py:24
  55.2 1.3 copy-start
  60.7 1.2 copy-start.9
  60.7 1.3 copy-start.23
  60.8 1.3 copy-start.26
  61.7 3.2 %copy-start.20 = (bf16[64,8,8,128]{3,2,1,0:T(8,128)(2,1)}, bf16[64,8,8,128]{3,2,1,0:T(8,128)(2,1)S(1)}, u32[]{:S(2)}) copy-start(bf16[64,8,8,128]{3,2,1,0:T(8,128)(2,1)S(1)} %fusion.78) | copy-start | bytes 3145732
  65.0 2.0 copy-start.2
  105.1 12.5 %copy-start.10 = (bf16[512,1024]{0,1:T(8,128)(2,1)S(1)}, bf16[512,1024]{0,1:T(8,128)(2,1)}, u32[]{:S(2)}) copy-start(bf16[512,1024]{0,1:T(8,128)(2,1)} %copy.213) | copy-start | bytes 3145732
  105.1 12.5 %copy-start.13 = (f32[8,128,512]{2,1,0:T(8,128)S(1)}, f32[8,128,512]{2,1,0:T(8,128)}, u32[]{:S(2)}) copy-start(f32[8,128,512]{2,1,0:T(8,128)} %fusion.42) | copy-start | bytes 6291460
  117.6 1.9 copy-start.16
  124.7 2.9 copy-start.25
  139.0 2.3 copy-start.29
  139.0 23.6 %copy-start.27 = (f32[8,512]{1,0:T(8,128)S(1)}, f32[8,512]{1,0:T(8,128)}, u32[]{:S(2)}) copy-start(f32[8,512]{1,0:T(8,128)} %bitcast_add_fusion) | copy-start | bytes 49156
  162.7 4.1 %copy-start.19 = (bf16[512,8,128]{0,2,1:T(8,128)(2,1)S(1)}, bf16[512,8,128]{0,2,1:T(8,128)(2,1)}, u32[]{:S(2)}) copy-start(bf16[512,8,128]{0,2,1:T(8,128)(2,1)} %copy.163) | copy-start | bytes 3145732
  166.7 2.3 copy-start.3
  166.7 2.3 copy-start.12
  166.7 2.5 copy-start.17
  169.7 1.3 copy-start.5
  173.1 4.4 %copy-start.4 = (bf16[8,512,512]{2,1,0:T(8,128)(2,1)S(1)}, bf16[8,512,512]{2,1,0:T(8,128)(2,1)}, u32[]{:S(2)}) copy-start(bf16[8,512,512]{2,1,0:T(8,128)(2,1)} %copy-done.3) | copy-start | bytes 12582916
  173.1 4.4 %copy-start.11 = (bf16[512,1024]{0,1:T(8,128)(2,1)S(1)}, bf16[512,1024]{0,1:T(8,128)(2,1)}, u32[]{:S(2)}) copy-start(bf16[512,1024]{0,1:T(8,128)(2,1)} %copy.213) | copy-start | bytes 3145732
  212.9 1.3 copy-start.6
  216.8 1.3 copy-start.7
  218.4 10.3 %collective-permute-start.1 = (f32[3,3,1024]{2,1,0:T(4,128)S(1)}, f32[3,3,1024]{2,1,0:T(4,128)S(1)}, u32[]{:S(2)}, u32[]{:S(2)}) collective-permute-start(f32[3,3,1024]{2,1,0:T(4,128)S(1)} %pad_maximum_fusion.3), channel_id=1, source_target_pairs={{2,0},{4,2},{6,4},{8,6},{10,8},{12,10},{14,12},{16,14},{18,16},{20... | collective-permute-start | bytes 110600 | tf_op jit(solution)/shard_map/ppermute | solution.py:16
  228.8 8.9 %copy-start.1 = (f32[515,1024]{1,0:T(8,128)S(1)}, f32[515,1024]{1,0:T(8,128)}, u32[]{:S(2)}) copy-start(f32[515,1024]{1,0:T(8,128)} %copy-done) | copy-start | bytes 6328324
  228.8 8.9 %copy-start.15 = (f32[512,1024]{1,0:T(8,128)S(1)}, f32[512,1024]{1,0:T(8,128)}, u32[]{:S(2)}) copy-start(f32[512,1024]{1,0:T(8,128)} %copy.176) | copy-start | bytes 6291460
  237.7 3.0 copy-start.14
Sparse Core Ops, SparseCore 0:
  27.6 77.4 all-gather.6
  144.1 48.9 all-gather.8
where the time goes:
time: 311 us; the launch traced here: 310 us
  blocking collectives  111 us (36%)
  other arithmetic  55.7 us (18%)
  waiting for transfers between devices  48.9 us (16%)
  matrix products  41.3 us (13%)
  local copies, waits for them, and re-layouts  34.1 us (11%)
  between operations  14.5 us (5%)
  starting transfers between devices  3.99 us (1%)
    psum x1, blocking collectives, body(): conv_grad, gain_grad = lax.psum((conv_part, gain_part), 'ctx')  59.3 us
    all_gather x1, waiting for transfers between devices, body(): lax.all_gather(device_sum[1][None], 'ctx', axis=0, tiled=True)  35.3 us
    all_gather x1, blocking collectives, body(): all_totals = lax.all_gather(device_sum[0][None], 'ctx', axis=0, tiled=True)  22.8 us
    all_gather x1, blocking collectives, prefix(): lax.all_gather(a.astype(kind), axis)  18.6 us
    add x15, other arithmetic, chain_step(): jnp.exp(later_part[0])[..., None, None] * earlier[1] + later_part[1]  16.6 us
    reduce_sum x3, other arithmetic, conv_backward(): jnp.sum(grad_rows * extended[TAPS - 1:TAPS - 1 + tok_here], axis=0)  14.7 us
    all_gather x1, waiting for transfers between devices, prefix(): lax.all_gather(a.astype(kind), axis)  13.5 us
    dot_general x1, matrix products, body(): jnp.einsum('nh,nhde->hde', factor_table, lax.all_gather(device_sum[1][Non...  12.5 us
  transfers between devices with their start and end apart: 4, of which 2 were waited for; matrix products, arithmetic and copies ran while one was open for 14% of the time, Pallas kernels for 0%

commit v1 on v0

--- a/solution.py
+++ b/solution.py
@@ -128,7 +128,12 @@
     )
     device_sum, before = local_chain(closing, blocks, False)
     zero_state = jnp.zeros((heads_here, HD, HD), jnp.float32)
-    all_totals = lax.all_gather(device_sum[0][None], "ctx", axis=0, tiled=True)
+    ring = [device_sum[0][None]]
+    for hop in range(15):
+        ring.append(lax.ppermute(ring[-1], "ctx", [(dev, (dev + 1) % 16) for dev in range(16)]))
+    all_totals = jnp.roll(
+        jnp.concatenate(ring[::-1], axis=0), (lax.axis_index("ctx") + 1) * ring[0].shape[0], axis=0
+    )
     device_index = lax.axis_index("ctx")
     cumulative = jnp.cumsum(all_totals, axis=0)
     before_me = cumulative[device_index] - all_totals[device_index]

time: 311 us -> 342 us (1.100)
  waiting for transfers between devices: 48.9 us -> 95.3 us
  blocking collectives: 111 us -> 87.1 us
    ppermute x0 -> x15, waiting for transfers between devices: none -> 80.7 us  [body(): lax.ppermute(ring[-1], 'ctx', [(dev, (dev + 1) % 16) for dev in range(16)])]
    all_gather x1, waiting for transfers between devices: 35.3 us -> 0.01 us  [body(): lax.all_gather(device_sum[1][None], 'ctx', axis=0, tiled=True)]
    all_gather x1 -> x0, blocking collectives: 22.8 us -> none  [body(): all_totals = lax.all_gather(device_sum[0][None], 'ctx', axis=0, tiled=True)]
    unnamed x3 -> x4, other arithmetic: 6.81 us -> 7.99 us
    unnamed x61 -> x83, local copies, waits for them, and re-layouts: 8.88 us -> 9.28 us
  transfers between devices with their start and end apart: 4 -> 19, of which waited for: 2 -> 16; matrix products, arithmetic and copies ran while one was open for 14% -> 14% of each run, Pallas kernels for 0% -> 0%
where the time goes in v1:
time: 342 us; the launch traced here: 340 us
  waiting for transfers between devices  95.3 us (28%)
  blocking collectives  87.1 us (25%)
  other arithmetic  58.2 us (17%)
  matrix products  41.2 us (12%)
  local copies, waits for them, and re-layouts  36.6 us (11%)
  between operations  14.6 us (4%)
  starting transfers between devices  6.68 us (2%)
    ppermute x15, waiting for transfers between devices, body(): lax.ppermute(ring[-1], 'ctx', [(dev, (dev + 1) % 16) for dev in range(16)])  80.7 us
    psum x1, blocking collectives, body(): conv_grad, gain_grad = lax.psum((conv_part, gain_part), 'ctx')  59.3 us
    all_gather x1, blocking collectives, prefix(): lax.all_gather(a.astype(kind), axis)  17 us
    add x15, other arithmetic, chain_step(): jnp.exp(later_part[0])[..., None, None] * earlier[1] + later_part[1]  16.6 us
    all_gather x1, waiting for transfers between devices, prefix(): lax.all_gather(a.astype(kind), axis)  14.6 us
    reduce_sum x3, other arithmetic, conv_backward(): jnp.sum(grad_rows * extended[TAPS - 1:TAPS - 1 + tok_here], axis=0)  14.4 us
    dot_general x1, matrix products, body(): jnp.einsum('nh,nhde->hde', factor_table, lax.all_gather(device_sum[1][Non...  12.5 us
    unnamed x83, local copies, waits for them, and re-layouts  9.28 us
  transfers between devices with their start and end apart: 19, of which 16 were waited for; matrix products, arithmetic and copies ran while one was open for 14% of the time, Pallas kernels for 0%

profile of v1, /device:TPU:0, one launch (start us, length us, event | category | flops | bytes accessed | tf_op | source)
XLA Modules:
  0.0 340.1 jit_solution(17409200392338837144)
XLA Ops:
  8.8 2.4 collective-permute-start
  11.2 2.2 reduce-window.6
  17.3 2.9 maximum_convert_fusion
  23.2 4.9 %fusion.49 = bf16[64,8,8,128]{3,2,1,0:T(8,128)(2,1)S(1)} fusion(f32[515,1024]{1,0:T(8,128)} %maximum_convert_fusion, f32[1024]{0:T(1024)S(1)} %bitcast.220, f32[1024]{0:T(1024)S(1)} %bitcast.222, f32[1024]{0:T(1024)S(1)} %bitcast.224, f32[1024]{0:T(1024)S(1)} %bitcast.218), kind=kLoop, calls=%fused_computation.94 | loop fusion | flops 4194304 | bytes 9453568
  29.5 2.7 collective-permute-start.1
  33.5 1.9 collective-permute-done.1
  35.4 5.7 %collective-permute-done.2 = f32[1,8]{1,0:T(1,128)S(1)} collective-permute-done((f32[1,8]{1,0:T(1,128)S(1)}, f32[1,8]{1,0:T(1,128)S(1)}, u32[]{:S(2)}, u32[]{:S(2)}) %collective-permute-start.2) | collective-permute-done | bytes 64 | tf_op jit(solution)/shard_map/ppermute | solution.py:133
  41.0 5.7 %collective-permute-done.3 = f32[1,8]{1,0:T(1,128)S(1)} collective-permute-done((f32[1,8]{1,0:T(1,128)S(1)}, f32[1,8]{1,0:T(1,128)S(1)}, u32[]{:S(2)}, u32[]{:S(2)}) %collective-permute-start.3) | collective-permute-done | bytes 64 | tf_op jit(solution)/shard_map/ppermute | solution.py:133
  46.7 5.7 %collective-permute-done.4 = f32[1,8]{1,0:T(1,128)S(1)} collective-permute-done((f32[1,8]{1,0:T(1,128)S(1)}, f32[1,8]{1,0:T(1,128)S(1)}, u32[]{:S(2)}, u32[]{:S(2)}) %collective-permute-start.4) | collective-permute-done | bytes 64 | tf_op jit(solution)/shard_map/ppermute | solution.py:133
  52.4 5.7 %collective-permute-done.5 = f32[1,8]{1,0:T(1,128)S(1)} collective-permute-done((f32[1,8]{1,0:T(1,128)S(1)}, f32[1,8]{1,0:T(1,128)S(1)}, u32[]{:S(2)}, u32[]{:S(2)}) %collective-permute-start.5) | collective-permute-done | bytes 64 | tf_op jit(solution)/shard_map/ppermute | solution.py:133
  58.1 5.7 %collective-permute-done.6 = f32[1,8]{1,0:T(1,128)S(1)} collective-permute-done((f32[1,8]{1,0:T(1,128)S(1)}, f32[1,8]{1,0:T(1,128)S(1)}, u32[]{:S(2)}, u32[]{:S(2)}) %collective-permute-start.6) | collective-permute-done | bytes 64 | tf_op jit(solution)/shard_map/ppermute | solution.py:133
  63.7 5.7 %collective-permute-done.7 = f32[1,8]{1,0:T(1,128)S(1)} collective-permute-done((f32[1,8]{1,0:T(1,128)S(1)}, f32[1,8]{1,0:T(1,128)S(1)}, u32[]{:S(2)}, u32[]{:S(2)}) %collective-permute-start.7) | collective-permute-done | bytes 64 | tf_op jit(solution)/shard_map/ppermute | solution.py:133
  69.4 5.7 %collective-permute-done.8 = f32[1,8]{1,0:T(1,128)S(1)} collective-permute-done((f32[1,8]{1,0:T(1,128)S(1)}, f32[1,8]{1,0:T(1,128)S(1)}, u32[]{:S(2)}, u32[]{:S(2)}) %collective-permute-start.8) | collective-permute-done | bytes 64 | tf_op jit(solution)/shard_map/ppermute | solution.py:133
  75.1 5.7 %collective-permute-done.9 = f32[1,8]{1,0:T(1,128)S(1)} collective-permute-done((f32[1,8]{1,0:T(1,128)S(1)}, f32[1,8]{1,0:T(1,128)S(1)}, u32[]{:S(2)}, u32[]{:S(2)}) %collective-permute-start.9) | collective-permute-done | bytes 64 | tf_op jit(solution)/shard_map/ppermute | solution.py:133
  80.7 5.7 %collective-permute-done.10 = f32[1,8]{1,0:T(1,128)S(1)} collective-permute-done((f32[1,8]{1,0:T(1,128)S(1)}, f32[1,8]{1,0:T(1,128)S(1)}, u32[]{:S(2)}, u32[]{:S(2)}) %collective-permute-start.10) | collective-permute-done | bytes 64 | tf_op jit(solution)/shard_map/ppermute | solution.py:133
  86.4 5.7 %collective-permute-done.11 = f32[1,8]{1,0:T(1,128)S(1)} collective-permute-done((f32[1,8]{1,0:T(1,128)S(1)}, f32[1,8]{1,0:T(1,128)S(1)}, u32[]{:S(2)}, u32[]{:S(2)}) %collective-permute-start.11) | collective-permute-done | bytes 64 | tf_op jit(solution)/shard_map/ppermute | solution.py:133
  92.1 5.7 %collective-permute-done.12 = f32[1,8]{1,0:T(1,128)S(1)} collective-permute-done((f32[1,8]{1,0:T(1,128)S(1)}, f32[1,8]{1,0:T(1,128)S(1)}, u32[]{:S(2)}, u32[]{:S(2)}) %collective-permute-start.12) | collective-permute-done | bytes 64 | tf_op jit(solution)/shard_map/ppermute | solution.py:133
  97.8 5.7 %collective-permute-done.13 = f32[1,8]{1,0:T(1,128)S(1)} collective-permute-done((f32[1,8]{1,0:T(1,128)S(1)}, f32[1,8]{1,0:T(1,128)S(1)}, u32[]{:S(2)}, u32[]{:S(2)}) %collective-permute-start.13) | collective-permute-done | bytes 64 | tf_op jit(solution)/shard_map/ppermute | solution.py:133
  103.4 5.7 %collective-permute-done.14 = f32[1,8]{1,0:T(1,128)S(1)} collective-permute-done((f32[1,8]{1,0:T(1,128)S(1)}, f32[1,8]{1,0:T(1,128)S(1)}, u32[]{:S(2)}, u32[]{:S(2)}) %collective-permute-start.14) | collective-permute-done | bytes 64 | tf_op jit(solution)/shard_map/ppermute | solution.py:133
  109.6 5.1 %collective-permute-done.15 = f32[1,8]{1,0:T(1,128)} collective-permute-done((f32[1,8]{1,0:T(1,128)S(1)}, f32[1,8]{1,0:T(1,128)}, u32[]{:S(2)}, u32[]{:S(2)}) %collective-permute-start.15) | collective-permute-done | bytes 64 | tf_op jit(solution)/shard_map/ppermute | solution.py:133
  114.7 2.9 concatenate.27
  124.4 2.3 copy.278
  127.9 2.9 multiply_convert_fusion.1
  130.9 2.0 copy-done.2
  132.8 2.8 fusion.42
  135.7 12.5 %fusion = f32[8,1,128,128]{3,1,2,0:T(1,128)S(1)} fusion(f32[16,8,1,1]{0,2,3,1:T(1,128)S(1)} %copy.272, f32[16,8,128,128]{3,2,1,0:T(8,128)} %bitcast.189), kind=kOutput, calls=%fused_computation.2 | convolution fusion | flops 25165824 | bytes 8913408 | tf_op jit(solution)/shard_map/nh,nhde->hde/dot_general | solution.py:146
  150.1 5.8 %psum.28 = f32[512]{0:T(512)S(1)} all-reduce(f32[512]{0:T(512)S(1)} %get-tuple-element.211), channel_id=1, replica_groups=mesh['ctx'=16,'head'=2] {'head'}, use_global_device_ids=true, to_apply=%region_4.5 | all-reduce | flops 512 | bytes 4096 | tf_op jit(solution)/shard_map/psum | solution.py:165
  155.9 2.9 copy.235
  158.8 2.6 fusion.7
  161.4 4.9 %psum.29 = f32[512]{0:T(512)S(1)} all-reduce(f32[512]{0:T(512)S(1)} %get-tuple-element.171), channel_id=1, replica_groups=mesh['ctx'=16,'head'=2] {'head'}, use_global_device_ids=true, to_apply=%region_6.7 | all-reduce | flops 512 | bytes 4096 | tf_op jit(solution)/shard_map/psum | solution.py:167
  166.4 3.9 %fusion.6 = (bf16[512,1024]{1,0:T(8,128)(2,1)}, bf16[512,1024]{1,0:T(8,128)(2,1)}) fusion(bf16[512,1024]{1,0:T(8,128)(2,1)} %param.15, f32[512,1024]{1,0:T(8,128)} %copy.235, f32[512]{0:T(512)S(1)} %multiply_multiply_fusion, f32[1024]{0:T(1024)S(1)} %copy-done.24, f32[512]{0:T(512)S(1)} %add_rsqrt_fusion), kind=kLoop, calls=%fused_computation.19 | loop fusion | flops 4718592 | bytes 5251072 | tf_op jit(solution)/shard_map/convert_element_type | solution.py:43
  170.2 2.3 copy.279
  172.5 2.7 fusion.39
  175.2 17.0 %all-gather.2 = bf16[16,1,8]{2,1,0:T(2,128)(2,1)S(1)} all-gather(bf16[1,1,8]{2,1,0:T(2,128)(2,1)S(1)} %copy-done.38), channel_id=1, replica_groups=mesh['ctx'=16,'head'=2] {'ctx'}, dimensions={0}, use_global_device_ids=true | all-gather | bytes 272 | tf_op jit(solution)/shard_map/all_gather | solution.py:24
  192.3 4.0 %multiply_convert_fusion = bf16[8,512,512]{2,1,0:T(8,128)(2,1)S(1)} fusion(f32[8,512]{1,0:T(8,128)} %bitcast_add_fusion.1, pred[512,512]{1,0:T(8,128)(4,1)S(1)} %iota_compare_fusion, bf16[512,8,128]{0,2,1:T(8,128)(2,1)} %bitcast.186, bf16[64,8,8,128]{3,2,1,0:T(8,128)(2,1)S(1)} %fusion.49), kind=kOutput, calls=%fused_computation.4 | convolution fusion | flops 547356672 | bytes 6569984 | tf_op jit(solution)/shard_map/nthe,nshe->nhts/dot_general | solution.py:176
  202.7 4.4 %fusion.65 = f32[8,128,512]{2,1,0:T(8,128)} fusion(bf16[512,8,128]{0,2,1:T(8,128)(2,1)S(1)} %bitcast.188, bf16[8,512,512]{2,1,0:T(8,128)(2,1)} %copy-done.2), kind=kOutput, calls=%fused_computation.142 | convolution fusion | flops 536870912 | bytes 7340032 | tf_op jit(solution)/shard_map/nhts,nthe->nshe/dot_general | solution.py:209
  207.1 2.0 fusion.64
  209.1 14.6 %all-gather.8.cloned.1.call-done = bf16[128,128,128]{2,1,0:T(8,128)(2,1)} async-done(((bf16[8,128,128]{2,1,0:T(8,128)(2,1)}), bf16[128,128,128]{2,1,0:T(8,128)(2,1)}) %all-gather.8.cloned.1.call-update) | async-done | bytes 4194320 | tf_op jit(solution)/shard_map/all_gather | solution.py:24
  223.8 17.3 %while.9 = (s32[]{:T(128)}, f32[8,128,128]{2,1,0:T(8,128)S(1)}, s32[]{:T(128)}, bf16[16,8]{1,0:T(8,128)(2,1)S(1)}, bf16[16,8,128,128]{3,2,1,0:T(8,128)(2,1)}, /*index=5*/s32[]{:T(128)}, s32[]{:T(128)}, s32[]{:T(128)}, s32[]{:T(128)}) while((s32[]{:T(128)}, f32[8,128,128]{2,1,0:T(8,128)S(1)}, s32[]{:T(128)}, bf16[16,8]{1,0:T(8,128)(2,1)S(1)}, ...), condition=%wide.region_8.9_spmd, body=%wide.region_7.8_spmd.sunk | while | flops 393230 | bytes 1310955 | solution.py:39
  241.1 2.4 fusion.35
  245.1 2.4 fusion.36
  250.7 2.9 copy.242
  253.6 2.9 copy.258
  256.5 2.9 copy.256
  259.5 8.5 %multiply_reduce_fusion.3 = (f32[1024]{0:T(1024)S(1)}, f32[1024]{0:T(1024)S(1)}, f32[1024]{0:T(1024)S(1)}, f32[1024]{0:T(1024)S(1)}, bf16[512,1024]{1,0:T(8,128)(2,1)}) fusion(f32[512,1024]{1,0:T(8,128)} %copy.258, f32[515,1024]{1,0:T(8,128)} %maximum_convert_fusion, f32[3,1024]{1,0:T(4,128)S(1)} %get-tuple-element.191, f32[1024]{0:T(1024)S(1)} %bitcast.221, ...), kind=kLoop, calls=%fused_computation.62 | loop fusion | flops 9957376 | bytes 11579392 | tf_op jit(solution)/shard_map/reduce_sum | solution.py:86
  268.0 2.9 multiply_reduce_fusion.11
  271.0 2.9 multiply_reduce_fusion.7
  274.0 59.3 %all-reduce = (f32[3,4,1024]{2,1,0:T(4,128)}, f32[1024]{0:T(1024)}) all-reduce(f32[3,4,1024]{2,1,0:T(4,128)S(1)} %pad_maximum_fusion.4, f32[1024]{0:T(1024)S(1)} %get-tuple-element.170), channel_id=1, replica_groups=mesh['ctx'=16,'head'=2] {'ctx'}, use_global_device_ids=true, to_apply=%region_21.22 | all-reduce | flops 13312 | bytes 106496 | tf_op jit(solution)/shard_map/psum | solution.py:231
  (180 shorter events, 49.6 us)
Async XLA Ops:
  7.2 13.0 %copy-start.21 = (bf16[512,1024]{1,0:T(8,128)(2,1)S(1)}, bf16[512,1024]{1,0:T(8,128)(2,1)}, u32[]{:S(2)}) copy-start(bf16[512,1024]{1,0:T(8,128)(2,1)} %param.10) | copy-start | bytes 3145732
  7.2 128.5 %all-gather.6.cloned.1.call-start = ((), (), s32[]{:S(2)}) async-start(), calls=%async_computation | async-start | bytes 8912896 | tf_op jit(solution)/shard_map/all_gather | solution.py:149
  8.8 8.5 %collective-permute-start = (bf16[3,3,1024]{2,1,0:T(4,128)(2,1)S(1)}, bf16[3,3,1024]{2,1,0:T(4,128)(2,1)S(1)}, u32[]{:S(2)}, u32[]{:S(2)}) collective-permute-start(bf16[3,3,1024]{2,1,0:T(4,128)(2,1)S(1)} %pad_maximum_fusion.5), channel_id=1, source_target_pairs={{0,2},{2,4},{4,6},{6,8},{8,10},{10,12},{12,14},{14,16},{16,18},{18... | collective-permute-start | bytes 55304 | tf_op jit(solution)/shard_map/ppermute | solution.py:16
  13.6 6.9 %copy-start.22 = (f32[8,4]{0,1:T(4,128)}, f32[8,4]{0,1:T(4,128)S(1)}, u32[]{:S(2)}) copy-start(f32[8,4]{0,1:T(4,128)S(1)} %slice_bitcast_fusion.9) | copy-start | bytes 388
  17.3 10.8 %copy-start.39 = (f32[8]{0:T(128)}, f32[8]{0:T(128)S(1)}, u32[]{:S(2)}) copy-start(f32[8]{0:T(128)S(1)} %get-tuple-element.210) | copy-start | bytes 100
  23.2 4.9 %copy-start.18 = (bf16[512,8,128]{0,2,1:T(8,128)(2,1)S(1)}, bf16[512,8,128]{0,2,1:T(8,128)(2,1)}, u32[]{:S(2)}) copy-start(bf16[512,8,128]{0,2,1:T(8,128)(2,1)} %copy.231) | copy-start | bytes 3145732
  28.1 164.2 %copy-start.8 = (bf16[64,8,8,128]{3,2,1,0:T(8,128)(2,1)}, bf16[64,8,8,128]{3,2,1,0:T(8,128)(2,1)S(1)}, u32[]{:S(2)}) copy-start(bf16[64,8,8,128]{3,2,1,0:T(8,128)(2,1)S(1)} %fusion.49) | copy-start | bytes 3145732
  28.1 4.7 %copy-start.23 = (f32[8,4]{0,1:T(4,128)S(1)}, f32[8,4]{0,1:T(4,128)}, u32[]{:S(2)}) copy-start(f32[8,4]{0,1:T(4,128)} %copy-done.22) | copy-start | bytes 388
  29.5 194.3 %all-gather.8.cloned.1.call-start = ((), (), s32[]{:S(2)}) async-start(), calls=%async_computation.1 | async-start | bytes 4456448 | tf_op jit(solution)/shard_map/all_gather | solution.py:24
  29.5 5.8 %collective-permute-start.1 = (f32[1,8]{1,0:T(1,128)}, f32[1,8]{1,0:T(1,128)S(1)}, u32[]{:S(2)}, u32[]{:S(2)}) collective-permute-start(f32[1,8]{1,0:T(1,128)} %bitcast.92), channel_id=1, source_target_pairs={{0,2},{2,4},{4,6},{6,8},{8,10},{10,12},{12,14},{14,16},{16,18},{18... | collective-permute-start | bytes 104 | tf_op jit(solution)/shard_map/ppermute | solution.py:133
  35.4 5.7 %collective-permute-start.2 = (f32[1,8]{1,0:T(1,128)S(1)}, f32[1,8]{1,0:T(1,128)S(1)}, u32[]{:S(2)}, u32[]{:S(2)}) collective-permute-start(f32[1,8]{1,0:T(1,128)S(1)} %collective-permute-done.1), channel_id=1, source_target_pairs={{0,2},{2,4},{4,6},{6,8},{8,10},{10,12},{12,14},{14,16},{16,18},{18... | collective-permute-start | bytes 104 | tf_op jit(solution)/shard_map/ppermute | solution.py:133
  41.0 5.7 %collective-permute-start.3 = (f32[1,8]{1,0:T(1,128)S(1)}, f32[1,8]{1,0:T(1,128)S(1)}, u32[]{:S(2)}, u32[]{:S(2)}) collective-permute-start(f32[1,8]{1,0:T(1,128)S(1)} %collective-permute-done.2), channel_id=1, source_target_pairs={{0,2},{2,4},{4,6},{6,8},{8,10},{10,12},{12,14},{14,16},{16,18},{18... | collective-permute-start | bytes 104 | tf_op jit(solution)/shard_map/ppermute | solution.py:133
  46.7 62.4 %copy-start.26 = (f32[1,8]{1,0:T(1,128)}, f32[1,8]{1,0:T(1,128)S(1)}, u32[]{:S(2)}) copy-start(f32[1,8]{1,0:T(1,128)S(1)} %collective-permute-done.3) | copy-start | bytes 100
  46.7 5.7 %collective-permute-start.4 = (f32[1,8]{1,0:T(1,128)S(1)}, f32[1,8]{1,0:T(1,128)S(1)}, u32[]{:S(2)}, u32[]{:S(2)}) collective-permute-start(f32[1,8]{1,0:T(1,128)S(1)} %collective-permute-done.3), channel_id=1, source_target_pairs={{0,2},{2,4},{4,6},{6,8},{8,10},{10,12},{12,14},{14,16},{16,18},{18... | collective-permute-start | bytes 104 | tf_op jit(solution)/shard_map/ppermute | solution.py:133
  52.4 56.7 %copy-start.27 = (f32[1,8]{1,0:T(1,128)}, f32[1,8]{1,0:T(1,128)S(1)}, u32[]{:S(2)}) copy-start(f32[1,8]{1,0:T(1,128)S(1)} %collective-permute-done.4) | copy-start | bytes 100
  52.4 5.7 %collective-permute-start.5 = (f32[1,8]{1,0:T(1,128)S(1)}, f32[1,8]{1,0:T(1,128)S(1)}, u32[]{:S(2)}, u32[]{:S(2)}) collective-permute-start(f32[1,8]{1,0:T(1,128)S(1)} %collective-permute-done.4), channel_id=1, source_target_pairs={{0,2},{2,4},{4,6},{6,8},{8,10},{10,12},{12,14},{14,16},{16,18},{18... | collective-permute-start | bytes 104 | tf_op jit(solution)/shard_map/ppermute | solution.py:133
  58.1 51.1 %copy-start.28 = (f32[1,8]{1,0:T(1,128)}, f32[1,8]{1,0:T(1,128)S(1)}, u32[]{:S(2)}) copy-start(f32[1,8]{1,0:T(1,128)S(1)} %collective-permute-done.5) | copy-start | bytes 100
  58.1 5.7 %collective-permute-start.6 = (f32[1,8]{1,0:T(1,128)S(1)}, f32[1,8]{1,0:T(1,128)S(1)}, u32[]{:S(2)}, u32[]{:S(2)}) collective-permute-start(f32[1,8]{1,0:T(1,128)S(1)} %collective-permute-done.5), channel_id=1, source_target_pairs={{0,2},{2,4},{4,6},{6,8},{8,10},{10,12},{12,14},{14,16},{16,18},{18... | collective-permute-start | bytes 104 | tf_op jit(solution)/shard_map/ppermute | solution.py:133
  63.7 45.4 %copy-start.29 = (f32[1,8]{1,0:T(1,128)}, f32[1,8]{1,0:T(1,128)S(1)}, u32[]{:S(2)}) copy-start(f32[1,8]{1,0:T(1,128)S(1)} %collective-permute-done.6) | copy-start | bytes 100
  63.7 5.7 %collective-permute-start.7 = (f32[1,8]{1,0:T(1,128)S(1)}, f32[1,8]{1,0:T(1,128)S(1)}, u32[]{:S(2)}, u32[]{:S(2)}) collective-permute-start(f32[1,8]{1,0:T(1,128)S(1)} %collective-permute-done.6), channel_id=1, source_target_pairs={{0,2},{2,4},{4,6},{6,8},{8,10},{10,12},{12,14},{14,16},{16,18},{18... | collective-permute-start | bytes 104 | tf_op jit(solution)/shard_map/ppermute | solution.py:133
  69.4 39.7 %copy-start.30 = (f32[1,8]{1,0:T(1,128)}, f32[1,8]{1,0:T(1,128)S(1)}, u32[]{:S(2)}) copy-start(f32[1,8]{1,0:T(1,128)S(1)} %collective-permute-done.7) | copy-start | bytes 100
  69.4 5.7 %collective-permute-start.8 = (f32[1,8]{1,0:T(1,128)S(1)}, f32[1,8]{1,0:T(1,128)S(1)}, u32[]{:S(2)}, u32[]{:S(2)}) collective-permute-start(f32[1,8]{1,0:T(1,128)S(1)} %collective-permute-done.7), channel_id=1, source_target_pairs={{0,2},{2,4},{4,6},{6,8},{8,10},{10,12},{12,14},{14,16},{16,18},{18... | collective-permute-start | bytes 104 | tf_op jit(solution)/shard_map/ppermute | solution.py:133
  75.1 34.1 %copy-start.31 = (f32[1,8]{1,0:T(1,128)}, f32[1,8]{1,0:T(1,128)S(1)}, u32[]{:S(2)}) copy-start(f32[1,8]{1,0:T(1,128)S(1)} %collective-permute-done.8) | copy-start | bytes 100
  75.1 5.7 %collective-permute-start.9 = (f32[1,8]{1,0:T(1,128)S(1)}, f32[1,8]{1,0:T(1,128)S(1)}, u32[]{:S(2)}, u32[]{:S(2)}) collective-permute-start(f32[1,8]{1,0:T(1,128)S(1)} %collective-permute-done.8), channel_id=1, source_target_pairs={{0,2},{2,4},{4,6},{6,8},{8,10},{10,12},{12,14},{14,16},{16,18},{18... | collective-permute-start | bytes 104 | tf_op jit(solution)/shard_map/ppermute | solution.py:133
  80.7 28.4 %copy-start.32 = (f32[1,8]{1,0:T(1,128)}, f32[1,8]{1,0:T(1,128)S(1)}, u32[]{:S(2)}) copy-start(f32[1,8]{1,0:T(1,128)S(1)} %collective-permute-done.9) | copy-start | bytes 100
  80.7 5.7 %collective-permute-start.10 = (f32[1,8]{1,0:T(1,128)S(1)}, f32[1,8]{1,0:T(1,128)S(1)}, u32[]{:S(2)}, u32[]{:S(2)}) collective-permute-start(f32[1,8]{1,0:T(1,128)S(1)} %collective-permute-done.9), channel_id=1, source_target_pairs={{0,2},{2,4},{4,6},{6,8},{8,10},{10,12},{12,14},{14,16},{16,18},{18... | collective-permute-start | bytes 104 | tf_op jit(solution)/shard_map/ppermute | solution.py:133
  86.4 22.8 %copy-start.33 = (f32[1,8]{1,0:T(1,128)}, f32[1,8]{1,0:T(1,128)S(1)}, u32[]{:S(2)}) copy-start(f32[1,8]{1,0:T(1,128)S(1)} %collective-permute-done.10) | copy-start | bytes 100
  86.4 5.7 %collective-permute-start.11 = (f32[1,8]{1,0:T(1,128)S(1)}, f32[1,8]{1,0:T(1,128)S(1)}, u32[]{:S(2)}, u32[]{:S(2)}) collective-permute-start(f32[1,8]{1,0:T(1,128)S(1)} %collective-permute-done.10), channel_id=1, source_target_pairs={{0,2},{2,4},{4,6},{6,8},{8,10},{10,12},{12,14},{14,16},{16,18},{18... | collective-permute-start | bytes 104 | tf_op jit(solution)/shard_map/ppermute | solution.py:133
  92.1 17.1 %copy-start.34 = (f32[1,8]{1,0:T(1,128)}, f32[1,8]{1,0:T(1,128)S(1)}, u32[]{:S(2)}) copy-start(f32[1,8]{1,0:T(1,128)S(1)} %collective-permute-done.11) | copy-start | bytes 100
  92.1 5.7 %collective-permute-start.12 = (f32[1,8]{1,0:T(1,128)S(1)}, f32[1,8]{1,0:T(1,128)S(1)}, u32[]{:S(2)}, u32[]{:S(2)}) collective-permute-start(f32[1,8]{1,0:T(1,128)S(1)} %collective-permute-done.11), channel_id=1, source_target_pairs={{0,2},{2,4},{4,6},{6,8},{8,10},{10,12},{12,14},{14,16},{16,18},{18... | collective-permute-start | bytes 104 | tf_op jit(solution)/shard_map/ppermute | solution.py:133
  97.8 11.4 %copy-start.35 = (f32[1,8]{1,0:T(1,128)}, f32[1,8]{1,0:T(1,128)S(1)}, u32[]{:S(2)}) copy-start(f32[1,8]{1,0:T(1,128)S(1)} %collective-permute-done.12) | copy-start | bytes 100
  97.8 5.7 %collective-permute-start.13 = (f32[1,8]{1,0:T(1,128)S(1)}, f32[1,8]{1,0:T(1,128)S(1)}, u32[]{:S(2)}, u32[]{:S(2)}) collective-permute-start(f32[1,8]{1,0:T(1,128)S(1)} %collective-permute-done.12), channel_id=1, source_target_pairs={{0,2},{2,4},{4,6},{6,8},{8,10},{10,12},{12,14},{14,16},{16,18},{18... | collective-permute-start | bytes 104 | tf_op jit(solution)/shard_map/ppermute | solution.py:133
  103.4 5.8 %copy-start.36 = (f32[1,8]{1,0:T(1,128)}, f32[1,8]{1,0:T(1,128)S(1)}, u32[]{:S(2)}) copy-start(f32[1,8]{1,0:T(1,128)S(1)} %collective-permute-done.13) | copy-start | bytes 100
  103.4 5.7 %collective-permute-start.14 = (f32[1,8]{1,0:T(1,128)S(1)}, f32[1,8]{1,0:T(1,128)S(1)}, u32[]{:S(2)}, u32[]{:S(2)}) collective-permute-start(f32[1,8]{1,0:T(1,128)S(1)} %collective-permute-done.13), channel_id=1, source_target_pairs={{0,2},{2,4},{4,6},{6,8},{8,10},{10,12},{12,14},{14,16},{16,18},{18... | collective-permute-start | bytes 104 | tf_op jit(solution)/shard_map/ppermute | solution.py:133
  109.1 5.6 %collective-permute-start.15 = (f32[1,8]{1,0:T(1,128)S(1)}, f32[1,8]{1,0:T(1,128)}, u32[]{:S(2)}, u32[]{:S(2)}) collective-permute-start(f32[1,8]{1,0:T(1,128)S(1)} %collective-permute-done.14), channel_id=1, source_target_pairs={{0,2},{2,4},{4,6},{6,8},{8,10},{10,12},{12,14},{14,16},{16,18},{18... | collective-permute-start | bytes 104 | tf_op jit(solution)/shard_map/ppermute | solution.py:133
  127.7 3.2 copy-start.20
  135.7 12.5 %copy-start.10 = (bf16[512,1024]{0,1:T(8,128)(2,1)S(1)}, bf16[512,1024]{0,1:T(8,128)(2,1)}, u32[]{:S(2)}) copy-start(bf16[512,1024]{0,1:T(8,128)(2,1)} %copy.278) | copy-start | bytes 3145732
  135.7 12.5 %copy-start.13 = (f32[8,128,512]{2,1,0:T(8,128)S(1)}, f32[8,128,512]{2,1,0:T(8,128)}, u32[]{:S(2)}) copy-start(f32[8,128,512]{2,1,0:T(8,128)} %fusion.42) | copy-start | bytes 6291460
  155.9 2.9 copy-start.24
  170.2 5.0 %copy-start.38 = (bf16[1,1,8]{2,1,0:T(2,128)(2,1)S(1)}, bf16[1,1,8]{2,1,0:T(2,128)(2,1)}, u32[]{:S(2)}) copy-start(bf16[1,1,8]{2,1,0:T(2,128)(2,1)} %get-tuple-element.209) | copy-start | bytes 52
  192.3 4.0 %copy-start.19 = (bf16[512,8,128]{0,2,1:T(8,128)(2,1)S(1)}, bf16[512,8,128]{0,2,1:T(8,128)(2,1)}, u32[]{:S(2)}) copy-start(bf16[512,8,128]{0,2,1:T(8,128)(2,1)} %copy.231) | copy-start | bytes 3145732
  196.3 2.5 copy-start.17
  202.7 4.4 %copy-start.4 = (bf16[8,512,512]{2,1,0:T(8,128)(2,1)S(1)}, bf16[8,512,512]{2,1,0:T(8,128)(2,1)}, u32[]{:S(2)}) copy-start(bf16[8,512,512]{2,1,0:T(8,128)(2,1)} %copy-done.3) | copy-start | bytes 12582916
  202.7 4.4 %copy-start.11 = (bf16[512,1024]{0,1:T(8,128)(2,1)S(1)}, bf16[512,1024]{0,1:T(8,128)(2,1)}, u32[]{:S(2)}) copy-start(bf16[512,1024]{0,1:T(8,128)(2,1)} %copy.278) | copy-start | bytes 3145732
  249.1 10.3 %collective-permute-start.16 = (f32[3,3,1024]{2,1,0:T(4,128)S(1)}, f32[3,3,1024]{2,1,0:T(4,128)S(1)}, u32[]{:S(2)}, u32[]{:S(2)}) collective-permute-start(f32[3,3,1024]{2,1,0:T(4,128)S(1)} %pad_maximum_fusion.3), channel_id=1, source_target_pairs={{2,0},{4,2},{6,4},{8,6},{10,8},{12,10},{14,12},{16,14},{18,16},{20... | collective-permute-start | bytes 110600 | tf_op jit(solution)/shard_map/ppermute | solution.py:16
  259.4 8.6 %copy-start.1 = (f32[515,1024]{1,0:T(8,128)S(1)}, f32[515,1024]{1,0:T(8,128)}, u32[]{:S(2)}) copy-start(f32[515,1024]{1,0:T(8,128)} %copy-done) | copy-start | bytes 6328324
  259.5 8.5 %copy-start.15 = (f32[512,1024]{1,0:T(8,128)S(1)}, f32[512,1024]{1,0:T(8,128)}, u32[]{:S(2)}) copy-start(f32[512,1024]{1,0:T(8,128)} %copy.242) | copy-start | bytes 6291460
  268.0 3.0 copy-start.14
  (12 other events, 18.4 us)
Sparse Core Ops, SparseCore 0:
  29.6 77.5 all-gather.5
  175.3 48.3 all-gather.7
